TPU v7x, 32 devices: a whole 2x2x4 slice. The times are simulated.
32 devices in a mesh: row: 8 (over z, y), col: 4 (over x, core).
Axes of the slice: x: 2, y: 2, z: 4, core: 2. Of those that a mesh axis runs over, the one named last changes fastest.
Arguments:
- momentum: float32 [8192, 8192], P('row', 'col'), may hold values from -6 to 6
- gradient: bfloat16 [8192, 8192], P('row', 'col'), may hold values from -6 to 6
- weight: bfloat16 [8192, 8192], P('row', 'col'), may hold values from -6 to 6
- right_start: float32 [8192, 512], P('col', 'row'), may hold values from -0.0625 to 0.0625
Outputs:
- new_momentum: float32 [8192, 8192], P('row', 'col')
- new_weight: bfloat16 [8192, 8192], P('row', 'col')
- new_right: float32 [8192, 512], P('col', 'row')
All inputs are finite; a program needn't handle non-finite values.
Results may differ from a plain program's by a relative error of at most 0.001.
Values sent between devices are 32-bit elements; how exact they have to be, the bound alone decides.
A program may use at most 128 MiB of HBM per device.

v0:
```python
import jax
import jax.numpy as jnp
from jax import lax
from jax.sharding import PartitionSpec as P

OUT_DIM = 8192
IN_DIM = 8192
RANK = 512
ITERS = 2


precise_mode = lax.Precision.HIGHEST
momentum_decay = 0.9
step_rate = 0.1
epsilon = 1e-06


def self_gram(rows):
    return lax.dot_general(rows, rows, (((0,), (0,)), ((), ())), precision=precise_mode)


def solve_rows(rows, gram_sum):
    triangle = jnp.linalg.cholesky(gram_sum)
    return jax.scipy.linalg.solve_triangular(triangle, rows.T, lower=True).T


def shards(momentum, gradient, weight, right_start):
    blended = momentum + gradient.astype(jnp.float32)
    right_full = lax.all_gather(right_start, "row", axis=1, tiled=True)
    right_shard = right_start
    for iteration in range(ITERS):
        partials = jnp.dot(blended, right_full, precision=precise_mode)
        left_sum = lax.psum(partials, "col")
        gram_sum = lax.psum(self_gram(left_sum), "row")
        left_rows = solve_rows(left_sum, gram_sum)
        transposed = lax.dot_general(
            blended, left_rows, (((0,), (0,)), ((), ())), precision=precise_mode
        )
        products = lax.psum_scatter(transposed, "row", scatter_dimension=1, tiled=True)
        squares = lax.psum(jnp.sum(products * products, axis=0, keepdims=True), "col")
        col_norms = jnp.sqrt(squares + epsilon)
        right_shard = products / col_norms
        products_full, norms_full = (
            lax.all_gather(products, "row", axis=1, tiled=True),
            lax.all_gather(col_norms, "row", axis=1, tiled=True),
        )
        right_full = products_full / norms_full
    outer_dims = (((1,), (1,)), ((), ()))
    feedback = lax.dot_general(left_rows, products_full, outer_dims, precision=precise_mode)
    new_momentum = blended - (1.0 - momentum_decay) * feedback
    scale_factor = step_rate * (OUT_DIM * IN_DIM / RANK) ** 0.5
    update = lax.dot_general(left_rows, right_full, outer_dims, precision=precise_mode)
    new_weight = (weight.astype(jnp.float32) - scale_factor * update).astype(jnp.bfloat16)
    return (new_momentum, new_weight, right_shard)


def solution(mesh):
    return jax.shard_map(
        shards,
        mesh=mesh,
        in_specs=(P("row", "col"), P("row", "col"), P("row", "col"), P("col", "row")),
        out_specs=(P("row", "col"), P("row", "col"), P("col", "row")),
        check_vma=False,
    )
```

profile of v0, /device:TPU:0, one launch (start us, length us, event | category | flops | bytes accessed | tf_op | source)
XLA Modules:
  0.0 1108.0 jit_solution(18200171401721009502)
XLA Ops:
  7.9 77.7 %all-gather.4.cloned.1.call-done = f32[2048,512]{0,1:T(8,128)} async-done(((f32[2048,64]{0,1:T(8,128)}), f32[2048,512]{0,1:T(8,128)}) %all-gather.4.cloned.1.call-update) | async-done | bytes 4194320 | tf_op jit(solution)/shard_map/all_gather | solution.py:29
  85.7 19.0 %fusion.95 = f32[1024,512]{1,0:T(8,128)} fusion(f32[2048,512]{0,1:T(8,128)} %all-gather.4.cloned.1.call-done, f32[1024,2048]{1,0:T(8,128)} %param.7, bf16[1024,2048]{1,0:T(8,128)(2,1)} %param.8), kind=kOutput, calls=%fused_computation.160 | convolution fusion | flops 12889096192 | bytes 18874368 | tf_op jit(solution)/shard_map/dot_general | solution.py:32
  104.7 50.0 %all-reduce.8.cloned.1.call-done = f32[1024,512]{1,0:T(8,128)} async-done(((f32[1024,512]{1,0:T(8,128)}), f32[1024,512]{1,0:T(8,128)}) %all-reduce.8.cloned.1.call-update) | async-done | bytes 2097168 | tf_op jit(solution)/shard_map/psum | solution.py:33
  154.7 6.7 fusion.98
  161.9 78.0 %all-reduce.10.cloned.1.call-done = f32[512,512]{0,1:T(8,128)} async-done(((f32[512,512]{0,1:T(8,128)}), f32[512,512]{0,1:T(8,128)}) %all-reduce.10.cloned.1.call-update) | async-done | bytes 1048592 | tf_op jit(solution)/shard_map/psum | solution.py:34
  244.0 11.7 %cholesky.286 = f32[128,128]{1,0:T(8,128)S(1)} custom-call(f32[128,128]{1,0:T(8,128)S(1)} %cholesky.426), custom_call_target="Cholesky" | custom-call | tf_op jit(solution)/shard_map/jit(cholesky)/cholesky | solution.py:23
  255.7 9.8 custom-call.27
  268.2 11.7 %cholesky.305 = f32[128,128]{1,0:T(8,128)S(1)} custom-call(f32[128,128]{1,0:T(8,128)S(1)} %cholesky.430), custom_call_target="Cholesky" | custom-call | tf_op jit(solution)/shard_map/jit(cholesky)/cholesky | solution.py:23
  279.9 10.0 custom-call.28
  291.5 11.7 %cholesky.326 = f32[128,128]{1,0:T(8,128)S(1)} custom-call(f32[128,128]{1,0:T(8,128)S(1)} %cholesky.435), custom_call_target="Cholesky" | custom-call | tf_op jit(solution)/shard_map/jit(cholesky)/cholesky | solution.py:23
  303.9 9.8 custom-call.29
  315.2 11.7 %cholesky.343 = f32[128,128]{1,0:T(8,128)S(1)} custom-call(f32[128,128]{1,0:T(8,128)S(1)} %convolution_subtract_fusion.9), custom_call_target="Cholesky" | custom-call | tf_op jit(solution)/shard_map/jit(cholesky)/cholesky | solution.py:23
  332.2 11.4 %while.4 = (s32[]{:T(128)}, f32[512,512]{1,0:T(8,128)}, s32[4,2]{0,1:T(2,128)S(1)}, f32[4,128,128]{2,1,0:T(8,128)S(1)}, s32[]{:T(128)}) while((s32[]{:T(128)}, f32[512,512]{1,0:T(8,128)}, s32[4,2]{0,1:T(2,128)S(1)}, f32[4,128,128]{2,1,0:T(8,128)S(1)}, s32[]{:T(128)}) %tuple.55), condition=%wide.while_cond, body=%wide.while_body.sunk | while | flops 2 | bytes 131189 | solution.py:24
  332.9 2.2 bitcast_dynamic-update-slice_fusion.5
  335.7 2.2 bitcast_dynamic-update-slice_fusion.5
  343.6 39.3 %custom-call.30 = f32[4,128,128]{1,2,0:T(8,128)S(1)} custom-call(f32[4,128,128]{2,1,0:T(8,128)S(1)} %get-tuple-element.19), custom_call_target="InvertDiagBlocksLowerTriangular" | custom-call | tf_op jit(solution)/shard_map/jit(_solve_triangular)/triangular_solve | solution.py:24
  386.1 3.0 convolution_subtract_fusion.1
  389.8 3.6 fusion.28
  394.1 17.4 %fusion.3 = f32[2048,512]{0,1:T(8,128)} fusion(f32[128,1024]{1,0:T(8,128)S(1)} %fusion.66, f32[128,1024]{1,0:T(8,128)S(1)} %fusion.67, f32[128,1024]{1,0:T(8,128)S(1)} %fusion.69, f32[128,1024]{1,0:T(8,128)S(1)} %fusion.41, f32[1024,2048]{1,0:T(8,128)} %param.7, bf16[1024,2048]{1,0:T(8,128)(2,1)S(1)} %copy-done), kind=kOutput, calls=%fused_computation.10 | convolution fusion | flops 12890669056 | bytes 18874368 | tf_op jit(solution)/shard_map/dot_general | solution.py:36
  411.5 88.0 %reduce-scatter.3.cloned.1.call-done = f32[2048,64]{0,1:T(8,128)} async-done(((f32[2048,512]{0,1:T(8,128)}), f32[2048,64]{0,1:T(8,128)}) %reduce-scatter.3.cloned.1.call-update) | async-done | bytes 524304 | tf_op jit(solution)/shard_map/reduce_scatter | solution.py:39
  502.0 6.2 psum.44
  508.3 21.6 %all-reduce.1 = f32[512]{0:T(512)S(1)} all-reduce(f32[512]{0:T(512)S(1)} %bitcast_dynamic-update-slice_fusion.2), channel_id=1, replica_groups=mesh['row'=8,'col'=4] {'row'}, use_global_device_ids=true, to_apply=%add.1 | all-reduce | flops 512 | bytes 4096
  529.9 44.4 %all-gather.6.cloned.1.call-done = f32[2048,512]{0,1:T(8,128)} async-done(((f32[2048,64]{0,1:T(8,128)}), f32[2048,512]{0,1:T(8,128)}) %all-gather.6.cloned.1.call-update) | async-done | bytes 4194320 | tf_op jit(solution)/shard_map/all_gather | solution.py:44
  574.3 19.7 %fusion.1 = f32[1024,512]{1,0:T(8,128)} fusion(f32[2048,512]{0,1:T(8,128)} %all-gather.6.cloned.1.call-done, f32[512]{0:T(512)S(1)} %all-reduce.1, f32[1024,2048]{1,0:T(8,128)} %param.7, bf16[1024,2048]{1,0:T(8,128)(2,1)} %param.8), kind=kOutput, calls=%fused_computation.8 | convolution fusion | flops 12890144768 | bytes 18876416 | tf_op jit(solution)/shard_map/dot_general | solution.py:32
  594.0 50.0 %all-reduce.12.cloned.1.call-done = f32[1024,512]{1,0:T(8,128)} async-done(((f32[1024,512]{1,0:T(8,128)}), f32[1024,512]{1,0:T(8,128)}) %all-reduce.12.cloned.1.call-update) | async-done | bytes 2097168 | tf_op jit(solution)/shard_map/psum | solution.py:33
  644.0 6.7 fusion.99
  651.2 78.0 %all-reduce.14.cloned.1.call-done = f32[512,512]{0,1:T(8,128)} async-done(((f32[512,512]{0,1:T(8,128)}), f32[512,512]{0,1:T(8,128)}) %all-reduce.14.cloned.1.call-update) | async-done | bytes 1048592 | tf_op jit(solution)/shard_map/psum | solution.py:34
  733.2 11.7 %cholesky.358 = f32[128,128]{1,0:T(8,128)S(1)} custom-call(f32[128,128]{1,0:T(8,128)S(1)} %cholesky.439), custom_call_target="Cholesky" | custom-call | tf_op jit(solution)/shard_map/jit(cholesky)/cholesky | solution.py:23
  745.6 9.8 custom-call.31
  758.1 11.7 %cholesky.377 = f32[128,128]{1,0:T(8,128)S(1)} custom-call(f32[128,128]{1,0:T(8,128)S(1)} %cholesky.443), custom_call_target="Cholesky" | custom-call | tf_op jit(solution)/shard_map/jit(cholesky)/cholesky | solution.py:23
  770.5 9.9 custom-call.32
  782.0 11.7 %cholesky.398 = f32[128,128]{1,0:T(8,128)S(1)} custom-call(f32[128,128]{1,0:T(8,128)S(1)} %cholesky.448), custom_call_target="Cholesky" | custom-call | tf_op jit(solution)/shard_map/jit(cholesky)/cholesky | solution.py:23
  794.4 9.8 custom-call.33
  805.7 11.7 %cholesky.415 = f32[128,128]{1,0:T(8,128)S(1)} custom-call(f32[128,128]{1,0:T(8,128)S(1)} %convolution_subtract_fusion.8), custom_call_target="Cholesky" | custom-call | tf_op jit(solution)/shard_map/jit(cholesky)/cholesky | solution.py:23
  821.9 11.5 %while.5 = (s32[]{:T(128)}, f32[512,512]{1,0:T(8,128)}, s32[4,2]{0,1:T(2,128)S(1)}, f32[4,128,128]{2,1,0:T(8,128)S(1)}, s32[]{:T(128)}) while((s32[]{:T(128)}, f32[512,512]{1,0:T(8,128)}, s32[4,2]{0,1:T(2,128)S(1)}, f32[4,128,128]{2,1,0:T(8,128)S(1)}, s32[]{:T(128)}) %tuple.79), condition=%wide.while_cond.clone, body=%wide.while_body.clone.sunk | while | flops 2 | bytes 131189 | solution.py:24
  822.5 2.3 bitcast_dynamic-update-slice_fusion.6
  825.4 2.3 bitcast_dynamic-update-slice_fusion.6
  828.3 2.3 bitcast_dynamic-update-slice_fusion.6
  833.4 39.3 %custom-call.34 = f32[4,128,128]{1,2,0:T(8,128)S(1)} custom-call(f32[4,128,128]{2,1,0:T(8,128)S(1)} %get-tuple-element.20), custom_call_target="InvertDiagBlocksLowerTriangular" | custom-call | tf_op jit(solution)/shard_map/jit(_solve_triangular)/triangular_solve | solution.py:24
  875.9 3.0 convolution_subtract_fusion
  879.6 3.8 fusion.25
  884.1 17.4 %fusion.43 = f32[2048,512]{0,1:T(8,128)} fusion(f32[128,1024]{1,0:T(8,128)S(1)} %fusion.60, f32[128,1024]{1,0:T(8,128)S(1)} %fusion.61, f32[128,1024]{1,0:T(8,128)S(1)} %fusion.63, f32[128,1024]{1,0:T(8,128)S(1)} %fusion.39, f32[1024,2048]{1,0:T(8,128)} %param.7, bf16[1024,2048]{1,0:T(8,128)(2,1)S(1)} %copy-done.1), kind=kOutput, calls=%fused_computation.68 | convolution fusion | flops 12890669056 | bytes 18874368 | tf_op jit(solution)/shard_map/dot_general | solution.py:36
  901.6 88.0 %reduce-scatter.5.cloned.1.call-done = f32[2048,64]{0,1:T(8,128)} async-done(((f32[2048,512]{0,1:T(8,128)}), f32[2048,64]{0,1:T(8,128)}) %reduce-scatter.5.cloned.1.call-update) | async-done | bytes 524304 | tf_op jit(solution)/shard_map/reduce_scatter | solution.py:39
  990.8 6.2 psum.47
  997.1 22.0 %all-reduce.2 = f32[512]{0:T(512)S(1)} all-reduce(f32[512]{0:T(512)S(1)} %fusion.94), channel_id=1, replica_groups=mesh['row'=8,'col'=4] {'row'}, use_global_device_ids=true, to_apply=%add.2 | all-reduce | flops 512 | bytes 4096
  1021.1 43.4 %all-gather.8.cloned.1.call-done = f32[2048,512]{0,1:T(8,128)} async-done(((f32[2048,64]{0,1:T(8,128)}), f32[2048,512]{0,1:T(8,128)}) %all-gather.8.cloned.1.call-update) | async-done | bytes 4194320 | tf_op jit(solution)/shard_map/all_gather | solution.py:44
  1064.5 19.7 %multiply_subtract_fusion = f32[1024,2048]{1,0:T(8,128)} fusion(f32[2048,512]{0,1:T(8,128)} %all-gather.8.cloned.1.call-done, f32[128,1024]{1,0:T(8,128)S(1)} %fusion.60, f32[128,1024]{1,0:T(8,128)S(1)} %copy-done.5, f32[128,1024]{1,0:T(8,128)S(1)} %fusion.63, f32[128,1024]{1,0:T(8,128)S(1)} %fusion.39, f32[1024,2048]{1,0:T(8,128)} %param.7, ...), kind=kOutput, calls=%fused_computation.5 | convolution fusion | flops 12894863360 | bytes 27262976 | tf_op jit(solution)/shard_map/dot_general | solution.py:49
  1084.2 17.1 %subtract_convert_fusion = bf16[1024,2048]{1,0:T(8,128)(2,1)} fusion(bf16[1024,2048]{1,0:T(8,128)(2,1)S(1)} %copy-done.9, f32[2048,512]{0,1:T(8,128)S(1)} %copy-done.6, f32[512]{0:T(512)S(1)} %all-reduce.2, f32[128,1024]{1,0:T(8,128)S(1)} %fusion.60, f32[128,1024]{1,0:T(8,128)S(1)} %copy-done.5, f32[128,1024]{1,0:T(8,128)S(1)} %fusion.63, ...), kind=kOutput, calls=%fused_computation.4 | convolution fusion | flops 12895911936 | bytes 14682112 | tf_op jit(solution)/shard_map/dot_general | solution.py:52
  (123 shorter events, 54.3 us)
Async XLA Ops:
  7.2 78.5 %all-gather.4.cloned.1.call-start = ((), (), s32[]{:S(2)}) async-start(), calls=%async_computation.2 | async-start | bytes 4718592 | tf_op jit(solution)/shard_map/all_gather | solution.py:29
  7.9 146.8 %all-reduce.8.cloned.1.call-start = ((), (), s32[]{:S(2)}) async-start(), calls=%async_computation.3 | async-start | bytes 4194304 | tf_op jit(solution)/shard_map/psum | solution.py:33
  104.6 135.3 %all-reduce.10.cloned.1.call-start = ((), (), s32[]{:S(2)}) async-start(), calls=%async_computation.4 | async-start | bytes 2097152 | tf_op jit(solution)/shard_map/psum | solution.py:34
  161.4 338.1 %reduce-scatter.3.cloned.1.call-start = ((), (), s32[]{:S(2)}) async-start(), calls=%async_computation.5 | async-start | bytes 4718592 | tf_op jit(solution)/shard_map/reduce_scatter | solution.py:39
  243.0 1.0 copy-start.8
  244.0 139.0 %copy-start.2 = (f32[1024,512]{1,0:T(8,128)S(1)}, f32[1024,512]{1,0:T(8,128)}, u32[]{:S(2)}) copy-start(f32[1024,512]{1,0:T(8,128)} %all-reduce.8.cloned.1.call-done) | copy-start | bytes 6291460
  385.5 8.6 copy-start
  411.4 88.1 %copy-start.10 = (u32[32]{0:T(128)S(1)}, u32[32]{0:T(128)}, u32[]{:S(2)}) copy-start(u32[32]{0:T(128)} %constant.134) | copy-start | bytes 388
  411.5 162.8 %all-gather.6.cloned.1.call-start = ((), (), s32[]{:S(2)}) async-start(), calls=%async_computation.6 | async-start | bytes 4718592 | tf_op jit(solution)/shard_map/all_gather | solution.py:44
  499.5 144.5 %all-reduce.12.cloned.1.call-start = ((), (), s32[]{:S(2)}) async-start(), calls=%async_computation.7 | async-start | bytes 4194304 | tf_op jit(solution)/shard_map/psum | solution.py:33
  594.0 135.3 %all-reduce.14.cloned.1.call-start = ((), (), s32[]{:S(2)}) async-start(), calls=%async_computation.8 | async-start | bytes 2097152 | tf_op jit(solution)/shard_map/psum | solution.py:34
  650.8 338.8 %reduce-scatter.5.cloned.1.call-start = ((), (), s32[]{:S(2)}) async-start(), calls=%async_computation.9 | async-start | bytes 4718592 | tf_op jit(solution)/shard_map/reduce_scatter | solution.py:39
  732.3 1.0 copy-start.7
  733.2 139.5 %copy-start.3 = (f32[1024,512]{1,0:T(8,128)S(1)}, f32[1024,512]{1,0:T(8,128)}, u32[]{:S(2)}) copy-start(f32[1024,512]{1,0:T(8,128)} %all-reduce.12.cloned.1.call-done) | copy-start | bytes 6291460
  875.2 8.8 copy-start.1
  879.6 4.5 copy-start.4
  901.5 163.0 %copy-start.5 = (f32[128,1024]{1,0:T(8,128)S(1)}, f32[128,1024]{1,0:T(8,128)}, u32[]{:S(2)}) copy-start(f32[128,1024]{1,0:T(8,128)} %copy-done.4) | copy-start | bytes 1572868
  901.5 162.9 %all-gather.8.cloned.1.call-start = ((), (), s32[]{:S(2)}) async-start(), calls=%async_computation.10 | async-start | bytes 4718592 | tf_op jit(solution)/shard_map/all_gather | solution.py:44
  1064.5 19.7 %copy-start.6 = (f32[2048,512]{0,1:T(8,128)S(1)}, f32[2048,512]{0,1:T(8,128)}, u32[]{:S(2)}) copy-start(f32[2048,512]{0,1:T(8,128)} %all-gather.8.cloned.1.call-done) | copy-start | bytes 12582916
  1064.5 19.7 %copy-start.9 = (bf16[1024,2048]{1,0:T(8,128)(2,1)S(1)}, bf16[1024,2048]{1,0:T(8,128)(2,1)}, u32[]{:S(2)}) copy-start(bf16[1024,2048]{1,0:T(8,128)(2,1)} %param.9) | copy-start | bytes 12582916
Sparse Core Ops, SparseCore 0:
  10.1 75.5 all-gather.3
  104.8 49.8 all-reduce.7
  161.5 78.3 all-reduce.9
  411.6 87.8 reduce-scatter.2
  501.5 72.7 all-gather.5
  594.1 49.8 all-reduce.11
  650.9 78.3 all-reduce.13
  901.7 87.8 reduce-scatter.4
  991.7 72.6 all-gather.7
where the time goes:
time: 1120 us; the launch traced here: 1110 us
  waiting for transfers between devices  598 us (53%)
  other arithmetic  247 us (22%)
  matrix products  157 us (14%)
  blocking collectives  56 us (5%)
  local copies, waits for them, and re-layouts  28.7 us (3%)
  between operations  20.2 us (2%)
    reduce_scatter x2, waiting for transfers between devices, shards(): lax.psum_scatter(transposed, 'row', scatter_dimension=1, tiled=True)  176 us
    another operation x29, other arithmetic, solve_rows(): triangle = jnp.linalg.cholesky(gram_sum)  158 us
    psum x2, waiting for transfers between devices, shards(): gram_sum = lax.psum(self_gram(left_sum), 'row')  156 us
    psum x2, waiting for transfers between devices, shards(): left_sum = lax.psum(partials, 'col')  100 us
    all_gather x2, waiting for transfers between devices, shards(): lax.all_gather(products, 'row', axis=1, tiled=True)  87.8 us
    another operation x5, other arithmetic, solve_rows(): return jax.scipy.linalg.solve_triangular(triangle, rows.T, lower=True).T  81.4 us
    all_gather x1, waiting for transfers between devices, shards(): right_full = lax.all_gather(right_start, 'row', axis=1, tiled=True)  77.7 us
    unnamed x2, blocking collectives  43.6 us
  transfers between devices with their start and end apart: 9, of which 9 were waited for; matrix products, arithmetic and copies ran while one was open for 0% of the time, Pallas kernels for 0%

commit v1 on v0

v1 whole, which is shorter than its diff:
```python
import jax
import jax.numpy as jnp
from jax import lax
from jax.sharding import PartitionSpec as P

ITERS = 2
BLOCK = 128


gram_mode = lax.Precision.HIGHEST
wide_mode = lax.Precision.HIGH
momentum_decay = 0.9
step_rate = 0.1
epsilon = 1e-06


def self_gram(rows):
    return lax.dot_general(rows, rows, (((0,), (0,)), ((), ())), precision=gram_mode)


def times_transposed(a, b):
    return lax.dot_general(a, b, (((1,), (1,)), ((), ())), precision=gram_mode)


def solve_rows(rows, gram_sum):
    rank = gram_sum.shape[0]
    block = min(BLOCK, rank)
    trailing = gram_sum
    rest = rows
    solved = []
    for at in range(0, rank, block):
        size = min(block, rank - at)
        corner = lax.linalg.cholesky(trailing[:size, :size], symmetrize_input=False)
        inverse = lax.linalg.triangular_solve(
            corner, jnp.eye(size, dtype=corner.dtype), left_side=True, lower=True
        )
        block_rows = times_transposed(rest[:, :size], inverse)
        solved.append(block_rows)
        if at + size < rank:
            panel = times_transposed(trailing[size:, :size], inverse)
            trailing = trailing[size:, size:] - times_transposed(panel, panel)
            rest = rest[:, size:] - times_transposed(block_rows, panel)
    return jnp.concatenate(solved, axis=1)


def shards(momentum, gradient, weight, right_start):
    rows_at, cols_at = lax.psum(1, "row"), lax.psum(1, "col")
    out_dim, in_dim = momentum.shape[0] * rows_at, momentum.shape[1] * cols_at
    rank = right_start.shape[1] * rows_at
    blended = momentum + gradient.astype(jnp.float32)
    right_full = lax.all_gather(right_start, "row", axis=1, tiled=True)
    right_shard = right_start
    for iteration in range(ITERS):
        partials = jnp.dot(blended, right_full, precision=wide_mode)
        left_sum = lax.psum(partials, "col")
        gram_sum = lax.psum(self_gram(left_sum), "row")
        left_rows = solve_rows(left_sum, gram_sum)
        transposed = lax.dot_general(
            blended, left_rows, (((0,), (0,)), ((), ())), precision=wide_mode
        )
        products = lax.psum_scatter(transposed, "row", scatter_dimension=1, tiled=True)
        squares = lax.psum(jnp.sum(products * products, axis=0, keepdims=True), "col")
        col_norms = jnp.sqrt(squares + epsilon)
        right_shard = products / col_norms
        products_full, norms_full = (
            lax.all_gather(products, "row", axis=1, tiled=True),
            lax.all_gather(col_norms, "row", axis=1, tiled=True),
        )
        right_full = products_full / norms_full
    outer_dims = (((1,), (1,)), ((), ()))
    feedback = lax.dot_general(left_rows, products_full, outer_dims, precision=wide_mode)
    new_momentum = blended - (1.0 - momentum_decay) * feedback
    scale_factor = step_rate * (out_dim * in_dim / rank) ** 0.5
    update = lax.dot_general(left_rows, right_full, outer_dims, precision=wide_mode)
    new_weight = (weight.astype(jnp.float32) - scale_factor * update).astype(jnp.bfloat16)
    return (new_momentum, new_weight, right_shard)


def solution(mesh):
    return jax.shard_map(
        shards,
        mesh=mesh,
        in_specs=(P("row", "col"), P("row", "col"), P("row", "col"), P("col", "row")),
        out_specs=(P("row", "col"), P("row", "col"), P("col", "row")),
        check_vma=False,
    )
```

time: 1120 us -> 975 us (0.87)
  other arithmetic: 247 us -> 188 us
  matrix products: 157 us -> 107 us
  local copies, waits for them, and re-layouts: 28.7 us -> 2.97 us
    another operation x34 -> x40, other arithmetic: 239 us -> 183 us  [the longest x24 99.1 us: solve_rows(): corner = lax.linalg.cholesky(trailing[:size, :size], symmetrize_input=False)]
    another operation x26 -> x8, matrix products: 33.2 us -> 2.28 us  [solve_rows(): lax.linalg.triangular_solve(corner, jnp.eye(size, dtype=corner.dtype), le...]
    another operation x35 -> x0, local copies, waits for them, and re-layouts: 23 us -> none  [the longest x27 22.7 us: solve_rows(): return jax.scipy.linalg.solve_triangular(triangle, rows.T, lower=True).T]
    dot_general x8 -> x34, matrix products: 124 us -> 105 us  [the longest x2 24.1 us: shards(): partials = jnp.dot(blended, right_full, precision=wide_mode)]
  transfers between devices with their start and end apart: 9 -> 9, of which waited for: 9 -> 9; matrix products, arithmetic and copies ran while one was open for 0% -> 1% of each run, Pallas kernels for 0% -> 0%
where the time goes in v1:
time: 975 us; the launch traced here: 969 us
  waiting for transfers between devices  599 us (61%)
  other arithmetic  188 us (19%)
  matrix products  107 us (11%)
  blocking collectives  55.5 us (6%)
  between operations  15.6 us (2%)
    reduce_scatter x2, waiting for transfers between devices, shards(): lax.psum_scatter(transposed, 'row', scatter_dimension=1, tiled=True)  176 us
    psum x2, waiting for transfers between devices, shards(): gram_sum = lax.psum(self_gram(left_sum), 'row')  156 us
    psum x2, waiting for transfers between devices, shards(): left_sum = lax.psum(partials, 'col')  100 us
    another operation x24, other arithmetic, solve_rows(): corner = lax.linalg.cholesky(trailing[:size, :size], symmetrize_input=False)  99.1 us
    all_gather x2, waiting for transfers between devices, shards(): lax.all_gather(products, 'row', axis=1, tiled=True)  88.2 us
    another operation x16, other arithmetic, solve_rows(): lax.linalg.triangular_solve(corner, jnp.eye(size, dtype=corner.dtype), le...  84.4 us
    all_gather x1, waiting for transfers between devices, shards(): right_full = lax.all_gather(right_start, 'row', axis=1, tiled=True)  77.7 us
    unnamed x2, blocking collectives  43.1 us
  transfers between devices with their start and end apart: 9, of which 9 were waited for; matrix products, arithmetic and copies ran while one was open for 1% of the time, Pallas kernels for 0%

profile of v1, /device:TPU:0, one launch (start us, length us, event | category | flops | bytes accessed | tf_op | source)
XLA Modules:
  0.0 969.1 jit_solution(15669869728964990464)
XLA Ops:
  7.9 77.7 %all-gather.4.cloned.1.call-done = f32[2048,512]{0,1:T(8,128)} async-done(((f32[2048,64]{0,1:T(8,128)}), f32[2048,512]{0,1:T(8,128)}) %all-gather.4.cloned.1.call-update) | async-done | bytes 4194320 | tf_op jit(solution)/shard_map/all_gather | solution.py:51
  85.7 12.0 %fusion.75 = f32[1024,512]{1,0:T(8,128)} fusion(f32[2048,512]{0,1:T(8,128)} %all-gather.4.cloned.1.call-done, f32[1024,2048]{1,0:T(8,128)} %param.7, bf16[1024,2048]{1,0:T(8,128)(2,1)} %param.8), kind=kOutput, calls=%fused_computation.122 | convolution fusion | flops 6446645248 | bytes 18874368 | tf_op jit(solution)/shard_map/dot_general | solution.py:54
  97.7 50.0 %all-reduce.7.cloned.1.call-done = f32[1024,512]{1,0:T(8,128)} async-done(((f32[1024,512]{1,0:T(8,128)}), f32[1024,512]{1,0:T(8,128)}) %all-reduce.7.cloned.1.call-update) | async-done | bytes 2097168 | tf_op jit(solution)/shard_map/psum | solution.py:55
  147.7 6.7 fusion.76
  154.7 78.3 %all-reduce.9.cloned.1.call-done = f32[512,512]{1,0:T(8,128)} async-done(((f32[512,512]{1,0:T(8,128)}), f32[512,512]{1,0:T(8,128)}) %all-reduce.9.cloned.1.call-update) | async-done | bytes 1048592 | tf_op jit(solution)/shard_map/psum | solution.py:56
  233.8 11.7 %custom-call.20 = f32[128,128]{1,0:T(8,128)S(1)} custom-call(f32[128,128]{1,0:T(8,128)S(1)} %slice.125), custom_call_target="Cholesky" | custom-call | tf_op jit(solution)/shard_map/cholesky/custom-call.1 | solution.py:33
  246.9 9.8 %custom-call.21 = f32[1,128,128]{1,2,0:T(8,128)S(1)} custom-call(f32[1,128,128]{2,1,0:T(8,128)S(1)} %fusion.50), custom_call_target="InvertDiagBlocksLowerTriangular" | custom-call | tf_op jit(solution)/shard_map/triangular_solve/custom-call.0 | solution.py:34
  257.0 1.3 fusion.44
  258.2 1.7 convolution_subtract_fusion.3
  259.9 11.7 %custom-call.22 = f32[128,128]{1,0:T(8,128)S(1)} custom-call(f32[128,128]{1,0:T(8,128)S(1)} %slice.130), custom_call_target="Cholesky" | custom-call | tf_op jit(solution)/shard_map/cholesky/custom-call.1 | solution.py:33
  273.0 10.2 %custom-call.23 = f32[1,128,128]{1,2,0:T(8,128)S(1)} custom-call(f32[1,128,128]{2,1,0:T(8,128)S(1)} %fusion.51), custom_call_target="InvertDiagBlocksLowerTriangular" | custom-call | tf_op jit(solution)/shard_map/triangular_solve/custom-call.0 | solution.py:34
  284.2 11.7 %custom-call.24 = f32[128,128]{1,0:T(8,128)S(1)} custom-call(f32[128,128]{1,0:T(8,128)S(1)} %slice.135), custom_call_target="Cholesky" | custom-call | tf_op jit(solution)/shard_map/cholesky/custom-call.1 | solution.py:33
  297.2 9.8 %custom-call.25 = f32[1,128,128]{1,2,0:T(8,128)S(1)} custom-call(f32[1,128,128]{2,1,0:T(8,128)S(1)} %fusion.52), custom_call_target="InvertDiagBlocksLowerTriangular" | custom-call | tf_op jit(solution)/shard_map/triangular_solve/custom-call.0 | solution.py:34
  307.9 11.7 %custom-call.26 = f32[128,128]{1,0:T(8,128)S(1)} custom-call(f32[128,128]{1,0:T(8,128)S(1)} %convolution_subtract_fusion.9), custom_call_target="Cholesky" | custom-call | tf_op jit(solution)/shard_map/cholesky/custom-call.1 | solution.py:33
  320.9 10.0 %custom-call.27 = f32[1,128,128]{1,2,0:T(8,128)S(1)} custom-call(f32[1,128,128]{2,1,0:T(8,128)S(1)} %fusion.53), custom_call_target="InvertDiagBlocksLowerTriangular" | custom-call | tf_op jit(solution)/shard_map/triangular_solve/custom-call.0 | solution.py:34
  331.8 1.9 slice_subtract_fusion.1
  334.4 1.1 convolution_subtract_fusion.1
  337.7 11.1 %fusion.3 = f32[2048,512]{0,1:T(8,128)} fusion(f32[1024,128]{0,1:T(8,128)S(1)} %fusion.77, f32[1024,128]{0,1:T(8,128)S(1)} %fusion.19, f32[1024,128]{0,1:T(8,128)S(1)} %fusion.21, f32[1024,128]{0,1:T(8,128)S(1)} %fusion.23, f32[1024,2048]{1,0:T(8,128)} %param.7, bf16[1024,2048]{1,0:T(8,128)(2,1)S(1)} %copy-done), kind=kOutput, calls=%fused_computation.6 | convolution fusion | flops 6448218112 | bytes 18874368 | tf_op jit(solution)/shard_map/dot_general | solution.py:58
  348.8 88.0 %reduce-scatter.3.cloned.1.call-done = f32[2048,64]{0,1:T(8,128)} async-done(((f32[2048,512]{0,1:T(8,128)}), f32[2048,64]{0,1:T(8,128)}) %reduce-scatter.3.cloned.1.call-update) | async-done | bytes 524304 | tf_op jit(solution)/shard_map/reduce_scatter | solution.py:61
  438.1 1.2 multiply_reduce_fusion.1
  439.3 6.2 psum.44
  445.6 21.6 %all-reduce = f32[512]{0:T(512)S(1)} all-reduce(f32[512]{0:T(512)S(1)} %bitcast_dynamic-update-slice_fusion), channel_id=1, replica_groups=mesh['row'=8,'col'=4] {'row'}, use_global_device_ids=true, to_apply=%add | all-reduce | flops 512 | bytes 4096
  467.2 44.4 %all-gather.6.cloned.1.call-done = f32[2048,512]{0,1:T(8,128)} async-done(((f32[2048,64]{0,1:T(8,128)}), f32[2048,512]{0,1:T(8,128)}) %all-gather.6.cloned.1.call-update) | async-done | bytes 4194320 | tf_op jit(solution)/shard_map/all_gather | solution.py:66
  511.6 12.2 %fusion.1 = f32[1024,512]{1,0:T(8,128)} fusion(f32[2048,512]{0,1:T(8,128)} %all-gather.6.cloned.1.call-done, f32[512]{0:T(512)S(1)} %all-reduce, f32[1024,2048]{1,0:T(8,128)} %param.7, bf16[1024,2048]{1,0:T(8,128)(2,1)} %param.8), kind=kOutput, calls=%fused_computation.4 | convolution fusion | flops 6447693824 | bytes 18876416 | tf_op jit(solution)/shard_map/dot_general | solution.py:54
  523.8 50.0 %all-reduce.11.cloned.1.call-done = f32[1024,512]{1,0:T(8,128)} async-done(((f32[1024,512]{1,0:T(8,128)}), f32[1024,512]{1,0:T(8,128)}) %all-reduce.11.cloned.1.call-update) | async-done | bytes 2097168 | tf_op jit(solution)/shard_map/psum | solution.py:55
  573.8 6.7 fusion.78
  581.0 78.1 %all-reduce.13.cloned.1.call-done = f32[512,512]{1,0:T(8,128)} async-done(((f32[512,512]{1,0:T(8,128)}), f32[512,512]{1,0:T(8,128)}) %all-reduce.13.cloned.1.call-update) | async-done | bytes 1048592 | tf_op jit(solution)/shard_map/psum | solution.py:56
  659.9 11.7 %custom-call.28 = f32[128,128]{1,0:T(8,128)S(1)} custom-call(f32[128,128]{1,0:T(8,128)S(1)} %slice.140), custom_call_target="Cholesky" | custom-call | tf_op jit(solution)/shard_map/cholesky/custom-call.1 | solution.py:33
  672.9 9.8 %custom-call.29 = f32[1,128,128]{1,2,0:T(8,128)S(1)} custom-call(f32[1,128,128]{2,1,0:T(8,128)S(1)} %fusion.54), custom_call_target="InvertDiagBlocksLowerTriangular" | custom-call | tf_op jit(solution)/shard_map/triangular_solve/custom-call.0 | solution.py:34
  683.1 1.3 fusion.42
  684.3 1.7 convolution_subtract_fusion.2
  686.1 11.7 %custom-call.30 = f32[128,128]{1,0:T(8,128)S(1)} custom-call(f32[128,128]{1,0:T(8,128)S(1)} %slice.145), custom_call_target="Cholesky" | custom-call | tf_op jit(solution)/shard_map/cholesky/custom-call.1 | solution.py:33
  699.1 10.0 %custom-call.31 = f32[1,128,128]{1,2,0:T(8,128)S(1)} custom-call(f32[1,128,128]{2,1,0:T(8,128)S(1)} %fusion.55), custom_call_target="InvertDiagBlocksLowerTriangular" | custom-call | tf_op jit(solution)/shard_map/triangular_solve/custom-call.0 | solution.py:34
  710.7 11.7 %custom-call.32 = f32[128,128]{1,0:T(8,128)S(1)} custom-call(f32[128,128]{1,0:T(8,128)S(1)} %slice.150), custom_call_target="Cholesky" | custom-call | tf_op jit(solution)/shard_map/cholesky/custom-call.1 | solution.py:33
  723.7 9.8 %custom-call.33 = f32[1,128,128]{1,2,0:T(8,128)S(1)} custom-call(f32[1,128,128]{2,1,0:T(8,128)S(1)} %fusion.56), custom_call_target="InvertDiagBlocksLowerTriangular" | custom-call | tf_op jit(solution)/shard_map/triangular_solve/custom-call.0 | solution.py:34
  734.4 11.7 %custom-call.34 = f32[128,128]{1,0:T(8,128)S(1)} custom-call(f32[128,128]{1,0:T(8,128)S(1)} %convolution_subtract_fusion.8), custom_call_target="Cholesky" | custom-call | tf_op jit(solution)/shard_map/cholesky/custom-call.1 | solution.py:33
  747.6 9.8 %custom-call.35 = f32[1,128,128]{1,2,0:T(8,128)S(1)} custom-call(f32[1,128,128]{2,1,0:T(8,128)S(1)} %fusion.57), custom_call_target="InvertDiagBlocksLowerTriangular" | custom-call | tf_op jit(solution)/shard_map/triangular_solve/custom-call.0 | solution.py:34
  757.7 1.4 fusion.17
  759.2 1.9 slice_subtract_fusion
  765.0 10.9 %fusion.25 = f32[2048,512]{0,1:T(8,128)} fusion(f32[1024,128]{0,1:T(8,128)S(1)} %fusion.79, f32[1024,128]{0,1:T(8,128)S(1)} %fusion.13, f32[1024,128]{0,1:T(8,128)S(1)} %fusion.15, f32[1024,128]{0,1:T(8,128)S(1)} %fusion.17, f32[1024,2048]{1,0:T(8,128)} %param.7, bf16[1024,2048]{1,0:T(8,128)(2,1)S(1)} %copy-done.1), kind=kOutput, calls=%fused_computation.43 | convolution fusion | flops 6448218112 | bytes 18874368 | tf_op jit(solution)/shard_map/dot_general | solution.py:58
  776.0 88.0 %reduce-scatter.5.cloned.1.call-done = f32[2048,64]{0,1:T(8,128)} async-done(((f32[2048,512]{0,1:T(8,128)}), f32[2048,64]{0,1:T(8,128)}) %reduce-scatter.5.cloned.1.call-update) | async-done | bytes 524304 | tf_op jit(solution)/shard_map/reduce_scatter | solution.py:61
  864.0 1.2 multiply_reduce_fusion
  865.2 6.2 psum.47
  871.5 21.6 %all-reduce.1 = f32[512]{0:T(512)S(1)} all-reduce(f32[512]{0:T(512)S(1)} %fusion.74), channel_id=1, replica_groups=mesh['row'=8,'col'=4] {'row'}, use_global_device_ids=true, to_apply=%add.1 | all-reduce | flops 512 | bytes 4096
  893.1 1.9 broadcast_divide_fusion
  895.0 43.9 %all-gather.8.cloned.1.call-done = f32[2048,512]{0,1:T(8,128)} async-done(((f32[2048,64]{0,1:T(8,128)}), f32[2048,512]{0,1:T(8,128)}) %all-gather.8.cloned.1.call-update) | async-done | bytes 4194320 | tf_op jit(solution)/shard_map/all_gather | solution.py:66
  938.9 13.9 %multiply_subtract_fusion = f32[1024,2048]{1,0:T(8,128)} fusion(f32[2048,512]{0,1:T(8,128)} %all-gather.8.cloned.1.call-done, f32[1024,128]{0,1:T(8,128)S(1)} %fusion.79, f32[1024,128]{0,1:T(8,128)S(1)} %fusion.13, f32[1024,128]{0,1:T(8,128)S(1)} %fusion.15, f32[1024,128]{0,1:T(8,128)S(1)} %fusion.17, f32[1024,2048]{1,0:T(8,128)} %param.7, ...), kind=kOutput, calls=%fused_computation.1 | convolution fusion | flops 6452412416 | bytes 27262976 | tf_op jit(solution)/shard_map/dot_general | solution.py:71
  952.8 9.3 subtract_convert_fusion
  (100 shorter events, 27.6 us)
Async XLA Ops:
  7.2 78.5 %all-gather.4.cloned.1.call-start = ((), (), s32[]{:S(2)}) async-start(), calls=%async_computation.2 | async-start | bytes 4718592 | tf_op jit(solution)/shard_map/all_gather | solution.py:51
  7.9 139.8 %all-reduce.7.cloned.1.call-start = ((), (), s32[]{:S(2)}) async-start(), calls=%async_computation.3 | async-start | bytes 4194304 | tf_op jit(solution)/shard_map/psum | solution.py:55
  97.7 135.3 %all-reduce.9.cloned.1.call-start = ((), (), s32[]{:S(2)}) async-start(), calls=%async_computation.4 | async-start | bytes 2097152 | tf_op jit(solution)/shard_map/psum | solution.py:56
  154.4 176.8 %copy-start.2 = (f32[1024,512]{1,0:T(8,128)S(1)}, f32[1024,512]{1,0:T(8,128)}, u32[]{:S(2)}) copy-start(f32[1024,512]{1,0:T(8,128)} %all-reduce.7.cloned.1.call-done) | copy-start | bytes 6291460
  154.4 282.4 %reduce-scatter.3.cloned.1.call-start = ((), (), s32[]{:S(2)}) async-start(), calls=%async_computation.5 | async-start | bytes 4718592 | tf_op jit(solution)/shard_map/reduce_scatter | solution.py:61
  333.7 3.9 copy-start
  348.7 88.2 %copy-start.9 = (u32[32]{0:T(128)S(1)}, u32[32]{0:T(128)}, u32[]{:S(2)}) copy-start(u32[32]{0:T(128)} %constant.27) | copy-start | bytes 388
  348.8 162.8 %all-gather.6.cloned.1.call-start = ((), (), s32[]{:S(2)}) async-start(), calls=%async_computation.6 | async-start | bytes 4718592 | tf_op jit(solution)/shard_map/all_gather | solution.py:66
  436.8 137.0 %all-reduce.11.cloned.1.call-start = ((), (), s32[]{:S(2)}) async-start(), calls=%async_computation.7 | async-start | bytes 4194304 | tf_op jit(solution)/shard_map/psum | solution.py:55
  523.8 135.3 %all-reduce.13.cloned.1.call-start = ((), (), s32[]{:S(2)}) async-start(), calls=%async_computation.8 | async-start | bytes 2097152 | tf_op jit(solution)/shard_map/psum | solution.py:56
  580.5 177.2 %copy-start.3 = (f32[1024,512]{1,0:T(8,128)S(1)}, f32[1024,512]{1,0:T(8,128)}, u32[]{:S(2)}) copy-start(f32[1024,512]{1,0:T(8,128)} %all-reduce.11.cloned.1.call-done) | copy-start | bytes 6291460
  580.5 283.5 %reduce-scatter.5.cloned.1.call-start = ((), (), s32[]{:S(2)}) async-start(), calls=%async_computation.9 | async-start | bytes 4718592 | tf_op jit(solution)/shard_map/reduce_scatter | solution.py:61
  683.0 26.3 %copy-start.5 = (f32[128,128]{1,0:T(8,128)}, f32[128,128]{1,0:T(8,128)S(1)}, u32[]{:S(2)}) copy-start(f32[128,128]{1,0:T(8,128)S(1)} %fusion.32) | copy-start | bytes 196612
  709.4 0.6 copy-start.6
  710.7 50.4 %copy-start.7 = (f32[128,128]{1,0:T(8,128)S(1)}, f32[128,128]{1,0:T(8,128)}, u32[]{:S(2)}) copy-start(f32[128,128]{1,0:T(8,128)} %copy-done.6) | copy-start | bytes 196612
  761.1 3.9 copy-start.1
  775.9 162.9 %all-gather.8.cloned.1.call-start = ((), (), s32[]{:S(2)}) async-start(), calls=%async_computation.10 | async-start | bytes 4718592 | tf_op jit(solution)/shard_map/all_gather | solution.py:66
  938.9 13.9 %copy-start.4 = (f32[2048,512]{0,1:T(8,128)S(1)}, f32[2048,512]{0,1:T(8,128)}, u32[]{:S(2)}) copy-start(f32[2048,512]{0,1:T(8,128)} %all-gather.8.cloned.1.call-done) | copy-start | bytes 12582916
  938.9 13.9 %copy-start.8 = (bf16[1024,2048]{1,0:T(8,128)(2,1)S(1)}, bf16[1024,2048]{1,0:T(8,128)(2,1)}, u32[]{:S(2)}) copy-start(bf16[1024,2048]{1,0:T(8,128)(2,1)} %param.9) | copy-start | bytes 12582916
Sparse Core Ops, SparseCore 0:
  10.1 75.5 all-gather.3
  97.8 49.9 all-reduce.6
  154.5 78.3 all-reduce.8
  348.9 87.8 reduce-scatter.2
  438.8 72.7 all-gather.5
  523.9 49.8 all-reduce.10
  580.6 78.3 all-reduce.12
  776.0 87.8 reduce-scatter.4
  866.1 72.6 all-gather.7
